TPU v7x, 32 devices: a whole 2x2x4 slice. The times are simulated.
32 devices in a mesh: probe: 16 (over z, y, core), strip: 2 (over x).
Axes of the slice: x: 2, y: 2, z: 4, core: 2. Of those that a mesh axis runs over, the one named last changes fastest.
Arguments:
- potential: float32 [2, 512, 2048], P(None, 'probe', 'strip'), may hold values from 0 to 2
- probe_wave: float32 [2, 256, 256], replicated, may hold values from -6 to 6
- offsets: int32 [2, 2, 96], P('strip'), may hold values from -128 to 896, as said below
- members: int32 [2, 16, 6], P('strip', 'probe'), may hold values from 0 to 95, as said below
- counts: int32 [2, 16], P('strip', 'probe'), may hold values from 1 to 6, as said below
- measured: float32 [2, 16, 6, 256, 256], P('strip', 'probe'), may hold values from 0 to 4
Outputs:
- potential_grad: float32 [2, 512, 2048], P(None, 'probe', 'strip')
Inputs may be any that keep to these rules, and one draw needn't show every extreme that they name: offsets[s, 0, p] is a window's first row, 0 to 256; offsets[s, 1, p] its first column counted from the strip's first column, -128 to 896; both ends of both ranges occur in every strip. `members`: every position of a strip is listed exactly once over that strip's groups; a group uses its first counts[s, g] entries. `counts`: in every strip some group uses all 6 slots and some group uses one.
All inputs are finite; a program needn't handle non-finite values.
Results may differ from a plain program's by a relative error of at most 0.00021.
Values sent between devices are 32-bit elements; how exact they have to be, the bound alone decides.
No kernel may reach another device: no remote copies, remote signals or barrier semaphores. Data moves between devices by JAX's collectives and lax.ppermute only.
A program may use at most 64 MiB of HBM per device.

v0:
```python
import math
import jax
import jax.numpy as jnp
from jax import lax
from jax.sharding import PartitionSpec as P

EDGE = 128
A_PROP = 0.1
LOSS_SCALE = 0.03125


def extended(value, sides, width):
    for axis, dim in sides:
        peers, length = (lax.axis_size(axis), value.shape[dim])
        up = [(i, (i + 1) % peers) for i in range(peers - 1)]
        down = [(j, i) for i, j in up]
        last = lax.slice_in_dim(value, length - width, length, axis=dim)
        initial = lax.slice_in_dim(value, 0, width, axis=dim)
        before = lax.ppermute(last, axis, up)
        after = lax.ppermute(initial, axis, down)
        value = jnp.concatenate([before, value, after], axis=dim)
    return value


def laplace(values):
    padded = jnp.pad(values, ((1, 1), (1, 1)))
    return (
        padded[2:, 1:-1] + padded[:-2, 1:-1] + padded[1:-1, 2:] + padded[1:-1, :-2] - 4.0 * values
    )


def propagate(real_part, imag_part):
    term_re, term_im = (real_part, imag_part)
    out_re, out_im = (real_part, imag_part)
    for degree in range(1, 5):
        lap_re = laplace(term_re)
        lap_im = laplace(term_im)
        term_re, term_im = (-A_PROP / degree * lap_im, A_PROP / degree * lap_re)
        out_re = out_re + term_re
        out_im = out_im + term_im
    return (out_re, out_im)


def exit_wave(window, probe_wave):
    real_part, imag_part = (probe_wave[0], probe_wave[1])
    for slice_index in range(window.shape[0]):
        phases = window[slice_index]
        cosine, sine_part = (jnp.cos(phases), jnp.sin(phases))
        real_part, imag_part = (
            real_part * cosine - imag_part * sine_part,
            real_part * sine_part + imag_part * cosine,
        )
        real_part, imag_part = propagate(real_part, imag_part)
    return (real_part, imag_part)


def dft_tables(window_size):
    indices = jnp.arange(window_size, dtype=jnp.int32)
    product = indices[:, None] * indices[None, :] % window_size
    angles = -2.0 * math.pi / window_size * product.astype(jnp.float32)
    normal_scale = 1.0 / math.sqrt(window_size)
    return (jnp.cos(angles) * normal_scale, jnp.sin(angles) * normal_scale)


def matmul(left_side, right_side):
    return jnp.dot(
        left_side, right_side, precision=lax.Precision.HIGHEST, preferred_element_type=jnp.float32
    )


def slot_loss(window, probe_wave, intensity_data, table_re, table_im):
    real_part, imag_part = exit_wave(window, probe_wave)
    inner_re = matmul(table_re, real_part) - matmul(table_im, imag_part)
    inner_im = matmul(table_re, imag_part) + matmul(table_im, real_part)
    far_re = matmul(inner_re, table_re) - matmul(inner_im, table_im)
    far_im = matmul(inner_re, table_im) + matmul(inner_im, table_re)
    intensity = far_re * far_re + far_im * far_im
    return LOSS_SCALE * jnp.sum((intensity - intensity_data) ** 2)


def split_edges(gradient, own_width):
    outgoing = jnp.concatenate([gradient[:, :, :EDGE], gradient[:, :, own_width + EDGE :]], axis=2)
    return (outgoing, gradient[:, :, EDGE : EDGE + own_width])


def add_edges(own_part, arrived, own_width):
    own_part = own_part.at[:, :, :EDGE].add(arrived[:, :, :EDGE])
    return own_part.at[:, :, own_width - EDGE :].add(arrived[:, :, 3 * EDGE :])


def shards(potential, probe_wave, offsets, members, counts, measured):
    own_width = potential.shape[2]
    widened = extended(potential, (("strip", 2),), EDGE)
    whole_object = lax.all_gather(widened, "probe", axis=1, tiled=True)
    window_size = probe_wave.shape[-1]
    table_re, table_im = dft_tables(window_size)
    anchor = jnp.zeros((), jnp.int32)
    loss_grad = jax.grad(slot_loss)

    def visit(slot_index, gradient):
        position = members[0, 0, slot_index]
        start_row = offsets[0, 0, position]
        start_column = offsets[0, 1, position] + EDGE
        window = lax.dynamic_slice(
            whole_object,
            (anchor, start_row, start_column),
            (whole_object.shape[0], window_size, window_size),
        )
        window_grad = loss_grad(window, probe_wave, measured[0, 0, slot_index], table_re, table_im)
        current = lax.dynamic_slice(gradient, (anchor, start_row, start_column), window.shape)
        return lax.dynamic_update_slice(
            gradient, current + window_grad, (anchor, start_row, start_column)
        )

    gradient = lax.fori_loop(0, counts[0, 0], visit, jnp.zeros(whole_object.shape, jnp.float32))
    outgoing, own_part = split_edges(gradient, own_width)
    arrived = extended(outgoing, (("strip", 2),), EDGE)
    folded = add_edges(own_part, arrived, own_width)
    return lax.psum_scatter(folded, "probe", scatter_dimension=1, tiled=True)


def solution(mesh):
    placed = (
        P(None, "probe", "strip"),
        P(),
        P("strip", None, None),
        P("strip", "probe", None),
        P("strip", "probe"),
        P("strip", "probe", None, None, None),
    )
    return jax.shard_map(
        shards, mesh=mesh, in_specs=placed, out_specs=P(None, "probe", "strip"), check_vma=False
    )
```

profile of v0, /device:TPU:0, one launch (start us, length us, event | category | flops | bytes accessed | tf_op | source)
XLA Modules:
  0.0 486.8 jit_solution(17927370276558367795)
XLA Ops:
  7.3 4.9 collective-permute-start
  13.8 4.2 collective-permute-done.1
  21.3 54.9 %all-gather.2.cloned.1.call-done = f32[2,512,1280]{2,0,1:T(2,128)} async-done(((f32[2,32,1280]{2,0,1:T(2,128)}), f32[2,512,1280]{2,0,1:T(2,128)}) %all-gather.2.cloned.1.call-update) | async-done | bytes 5242896 | tf_op jit(solution)/shard_map/all_gather | solution.py:94
  76.2 2.7 broadcast_in_dim.28.clone
  79.0 308.3 %while.17 = (s32[]{:T(128)}, f32[2,512,1280]{2,1,0:T(8,128)}, s32[]{:T(128)}, s32[1,1,6]{2,1,0:T(1,128)S(1)}, s32[1,2,96]{2,1,0:T(2,128)S(1)}, /*index=5*/f32[2,...) while((s32[]{:T(128)}, f32[2,512,1280]{2,1,0:T(8,128)}, ...), condition=%wide.region_1.2_spmd.clone.clone, body=%wide.region_0.1_spmd.clone.clone.sunk | while | flops 3259498496 | bytes 60293496 | solution.py:115
  85.9 2.6 fusion.321
  105.8 2.5 add_multiply_fusion.3
  123.6 6.6 %dynamic_update_slice.10 = f32[2,512,1280]{2,1,0:T(8,128)} dynamic-update-slice(f32[2,512,1280]{2,1,0:T(8,128)} %get-tuple-element.599, f32[2,256,256]{2,1,0:T(8,128)S(1)} %copy.35, s32[]{:T(128)} %constant.243.clone.1..sunk, s32[]{:T(128)S(6)} %select_n.157, s32[]{:T(128)S(6)} %select_n.158) | dynamic-update-slice | bytes 1048580 | tf_op jit(solution)/shard_map/while/body/dynamic_update_slice | solution.py:111
  137.2 2.6 fusion.321
  157.1 2.5 add_multiply_fusion.3
  174.9 6.4 %dynamic_update_slice.10 = f32[2,512,1280]{2,1,0:T(8,128)} dynamic-update-slice(f32[2,512,1280]{2,1,0:T(8,128)} %get-tuple-element.599, f32[2,256,256]{2,1,0:T(8,128)S(1)} %copy.35, s32[]{:T(128)} %constant.243.clone.1..sunk, s32[]{:T(128)S(6)} %select_n.157, s32[]{:T(128)S(6)} %select_n.158) | dynamic-update-slice | bytes 1048580 | tf_op jit(solution)/shard_map/while/body/dynamic_update_slice | solution.py:111
  188.2 2.7 fusion.321
  208.3 2.5 add_multiply_fusion.3
  226.2 6.1 %dynamic_update_slice.10 = f32[2,512,1280]{2,1,0:T(8,128)} dynamic-update-slice(f32[2,512,1280]{2,1,0:T(8,128)} %get-tuple-element.599, f32[2,256,256]{2,1,0:T(8,128)S(1)} %copy.35, s32[]{:T(128)} %constant.243.clone.1..sunk, s32[]{:T(128)S(6)} %select_n.157, s32[]{:T(128)S(6)} %select_n.158) | dynamic-update-slice | bytes 1048580 | tf_op jit(solution)/shard_map/while/body/dynamic_update_slice | solution.py:111
  239.2 2.7 fusion.321
  259.2 2.5 add_multiply_fusion.3
  277.1 6.6 %dynamic_update_slice.10 = f32[2,512,1280]{2,1,0:T(8,128)} dynamic-update-slice(f32[2,512,1280]{2,1,0:T(8,128)} %get-tuple-element.599, f32[2,256,256]{2,1,0:T(8,128)S(1)} %copy.35, s32[]{:T(128)} %constant.243.clone.1..sunk, s32[]{:T(128)S(6)} %select_n.157, s32[]{:T(128)S(6)} %select_n.158) | dynamic-update-slice | bytes 1048580 | tf_op jit(solution)/shard_map/while/body/dynamic_update_slice | solution.py:111
  290.7 2.7 fusion.321
  310.7 2.5 add_multiply_fusion.3
  328.6 6.5 %dynamic_update_slice.10 = f32[2,512,1280]{2,1,0:T(8,128)} dynamic-update-slice(f32[2,512,1280]{2,1,0:T(8,128)} %get-tuple-element.599, f32[2,256,256]{2,1,0:T(8,128)S(1)} %copy.35, s32[]{:T(128)} %constant.243.clone.1..sunk, s32[]{:T(128)S(6)} %select_n.157, s32[]{:T(128)S(6)} %select_n.158) | dynamic-update-slice | bytes 1048580 | tf_op jit(solution)/shard_map/while/body/dynamic_update_slice | solution.py:111
  342.0 2.7 fusion.321
  379.9 6.7 %dynamic_update_slice.10 = f32[2,512,1280]{2,1,0:T(8,128)} dynamic-update-slice(f32[2,512,1280]{2,1,0:T(8,128)} %get-tuple-element.599, f32[2,256,256]{2,1,0:T(8,128)S(1)} %copy.35, s32[]{:T(128)} %constant.243.clone.1..sunk, s32[]{:T(128)S(6)} %select_n.157, s32[]{:T(128)S(6)} %select_n.158) | dynamic-update-slice | bytes 1048580 | tf_op jit(solution)/shard_map/while/body/dynamic_update_slice | solution.py:111
  391.1 4.7 slice.622
  402.9 77.1 %reduce-scatter.2.cloned.1.call-done = f32[2,32,1024]{2,1,0:T(8,128)} async-done(((f32[2,512,1024]{2,1,0:T(8,128)}), f32[2,32,1024]{2,1,0:T(8,128)}) %reduce-scatter.2.cloned.1.call-update) | async-done | bytes 262160 | tf_op jit(solution)/shard_map/reduce_scatter | solution.py:119
  (334 shorter events, 220.9 us)
Async XLA Ops:
  6.5 72.4 %copy-start.1 = (s32[1,1,6]{2,1,0:T(1,128)S(1)}, s32[1,1,6]{2,1,0:T(1,128)}, u32[]{:S(2)}) copy-start(s32[1,1,6]{2,1,0:T(1,128)} %param.15) | copy-start | bytes 76
  6.5 72.4 %copy-start = (s32[1,2,96]{2,1,0:T(2,128)S(1)}, s32[1,2,96]{2,1,0:T(2,128)}, u32[]{:S(2)}) copy-start(s32[1,2,96]{2,1,0:T(2,128)} %param.14) | copy-start | bytes 2308
  6.5 69.7 %all-gather.2.cloned.1.call-start = ((), (), s32[]{:S(2)}) async-start(), calls=%async_computation.1 | async-start | bytes 5570560 | tf_op jit(solution)/shard_map/all_gather | solution.py:94
  7.3 6.4 %collective-permute-start = (f32[2,32,128]{2,1,0:T(8,128)S(1)}, f32[2,32,128]{2,1,0:T(8,128)S(1)}, u32[]{:S(2)}, u32[]{:S(2)}) collective-permute-start(f32[2,32,128]{2,1,0:T(8,128)S(1)} %get-tuple-element.418), channel_id=1, source_target_pairs={{0,1},{2,3},{4,5},{6,7},{8,9},{10,11},{12,13},{14,15},{16,17},{18,... | collective-permute-start | bytes 98312 | tf_op jit(solution)/shard_map/ppermute | solution.py:19
  12.2 5.8 %collective-permute-start.1 = (f32[2,32,128]{2,1,0:T(8,128)S(1)}, f32[2,32,128]{2,1,0:T(8,128)S(1)}, u32[]{:S(2)}, u32[]{:S(2)}) collective-permute-start(f32[2,32,128]{2,1,0:T(8,128)S(1)} %get-tuple-element.419), channel_id=1, source_target_pairs={{1,0},{3,2},{5,4},{7,6},{9,8},{11,10},{13,12},{15,14},{17,16},{19,... | collective-permute-start | bytes 98312 | tf_op jit(solution)/shard_map/ppermute | solution.py:20
  20.0 460.0 %reduce-scatter.2.cloned.1.call-start = ((), (), s32[]{:S(2)}) async-start(), calls=%async_computation.2 | async-start | bytes 4456448 | tf_op jit(solution)/shard_map/reduce_scatter | solution.py:119
  388.5 8.0 %collective-permute-start.2 = (f32[2,512,128]{2,1,0:T(8,128)S(1)}, f32[2,512,128]{2,1,0:T(8,128)S(1)}, u32[]{:S(2)}, u32[]{:S(2)}) collective-permute-start(f32[2,512,128]{2,1,0:T(8,128)S(1)} %get-tuple-element.417), channel_id=1, source_target_pairs={{0,1},{2,3},{4,5},{6,7},{8,9},{10,11},{12,13},{14,15},{16,17},{18,... | collective-permute-start | bytes 1572872 | tf_op jit(solution)/shard_map/ppermute | solution.py:19
  389.8 11.1 %collective-permute-start.3 = (f32[2,512,128]{2,1,0:T(8,128)S(1)}, f32[2,512,128]{2,1,0:T(8,128)S(1)}, u32[]{:S(2)}, u32[]{:S(2)}) collective-permute-start(f32[2,512,128]{2,1,0:T(8,128)S(1)} %get-tuple-element.416), channel_id=1, source_target_pairs={{1,0},{3,2},{5,4},{7,6},{9,8},{11,10},{13,12},{15,14},{17,16},{19,... | collective-permute-start | bytes 1572872 | tf_op jit(solution)/shard_map/ppermute | solution.py:20
Sparse Core Ops, SparseCore 0:
  20.1 56.0 all-gather.1
  403.1 76.8 reduce-scatter.1
where the time goes:
time: 489 us; the launch traced here: 487 us
  matrix products  143 us (29%)
  waiting for transfers between devices  140 us (29%)
  local copies, waits for them, and re-layouts  98 us (20%)
  other arithmetic  47.6 us (10%)
  loops' own time  36.7 us (8%)
  between operations  13.5 us (3%)
  starting transfers between devices  8.81 us (2%)
    dot_general x96, matrix products, matmul(): jnp.dot(left_side, right_side, precision=lax.Precision.HIGHEST, preferred...  143 us
    reduce_scatter x1, waiting for transfers between devices, shards(): return lax.psum_scatter(folded, 'probe', scatter_dimension=1, tiled=True)  77.1 us
    all_gather x1, waiting for transfers between devices, shards(): whole_object = lax.all_gather(widened, 'probe', axis=1, tiled=True)  54.9 us
    dynamic_update_slice x12, local copies, waits for them, and re-layouts, visit(): lax.dynamic_update_slice(gradient, current + window_grad, (anchor, start_...  40.1 us
    another operation x1, loops' own time, shards(): lax.fori_loop(0, counts[0, 0], visit, jnp.zeros(whole_object.shape, jnp.f...  36.7 us
    mul x120, other arithmetic, propagate(): term_re, term_im = (-A_PROP / degree * lap_im, A_PROP / degree * lap_re)  29.8 us
    slice x6, local copies, waits for them, and re-layouts, exit_wave(): phases = window[slice_index]  16 us
  transfers between devices with their start and end apart: 6, of which 6 were waited for; matrix products, arithmetic and copies ran while one was open for 2% of the time, Pallas kernels for 0%

commit v1 on v0

--- a/solution.py
+++ b/solution.py
@@ -91,7 +91,14 @@
 def shards(potential, probe_wave, offsets, members, counts, measured):
     own_width = potential.shape[2]
     widened = extended(potential, (("strip", 2),), EDGE)
-    whole_object = lax.all_gather(widened, "probe", axis=1, tiled=True)
+    ring = [widened]
+    for hop in range(15):
+        ring.append(lax.ppermute(ring[-1], "probe", [(dev, (dev + 1) % 16) for dev in range(16)]))
+    whole_object = jnp.roll(
+        jnp.concatenate(ring[::-1], axis=1),
+        (lax.axis_index("probe") + 1) * ring[0].shape[1],
+        axis=1,
+    )
     window_size = probe_wave.shape[-1]
     table_re, table_im = dft_tables(window_size)
     anchor = jnp.zeros((), jnp.int32)

time: 489 us -> 614 us (1.26)
  waiting for transfers between devices: 140 us -> 213 us
  loops' own time: 36.7 us -> 59.1 us
  other arithmetic: 47.6 us -> 65.6 us
    ppermute x0 -> x15, waiting for transfers between devices: none -> 137 us  [shards(): lax.ppermute(ring[-1], 'probe', [(dev, (dev + 1) % 16) for dev in range(1...]
    all_gather x1 -> x0, waiting for transfers between devices: 54.9 us -> none  [shards(): whole_object = lax.all_gather(widened, 'probe', axis=1, tiled=True)]
    another operation x1, loops' own time: 36.7 us -> 59.1 us  [shards(): lax.fori_loop(0, counts[0, 0], visit, jnp.zeros(whole_object.shape, jnp.f...]
    unnamed x5 -> x62, local copies, waits for them, and re-layouts: 1.25 us -> 13.7 us
    add x12, other arithmetic: 3.49 us -> 13 us  [exit_wave(): real_part * sine_part + imag_part * cosine]
    mul x120, other arithmetic: 29.8 us -> 38.5 us  [propagate(): term_re, term_im = (-A_PROP / degree * lap_im, A_PROP / degree * lap_re)]
    reduce_scatter x1, waiting for transfers between devices: 77.1 us -> 68.8 us  [shards(): return lax.psum_scatter(folded, 'probe', scatter_dimension=1, tiled=True)]
    slice x6, local copies, waits for them, and re-layouts: 16 us -> 8.05 us  [exit_wave(): phases = window[slice_index]]
  transfers between devices with their start and end apart: 6 -> 20, of which waited for: 6 -> 20; matrix products, arithmetic and copies ran while one was open for 2% -> 1% of each run, Pallas kernels for 0% -> 0%
where the time goes in v1:
time: 614 us; the launch traced here: 608 us
  waiting for transfers between devices  213 us (35%)
  matrix products  143 us (23%)
  local copies, waits for them, and re-layouts  104 us (17%)
  other arithmetic  65.6 us (11%)
  loops' own time  59.1 us (10%)
  between operations  14.2 us (2%)
  starting transfers between devices  8.86 us (1%)
    dot_general x96, matrix products, matmul(): jnp.dot(left_side, right_side, precision=lax.Precision.HIGHEST, preferred...  143 us
    ppermute x15, waiting for transfers between devices, shards(): lax.ppermute(ring[-1], 'probe', [(dev, (dev + 1) % 16) for dev in range(1...  137 us
    reduce_scatter x1, waiting for transfers between devices, shards(): return lax.psum_scatter(folded, 'probe', scatter_dimension=1, tiled=True)  68.8 us
    another operation x1, loops' own time, shards(): lax.fori_loop(0, counts[0, 0], visit, jnp.zeros(whole_object.shape, jnp.f...  59.1 us
    dynamic_update_slice x12, local copies, waits for them, and re-layouts, visit(): lax.dynamic_update_slice(gradient, current + window_grad, (anchor, start_...  40.1 us
    mul x120, other arithmetic, propagate(): term_re, term_im = (-A_PROP / degree * lap_im, A_PROP / degree * lap_re)  38.5 us
    unnamed x62, local copies, waits for them, and re-layouts  13.7 us
    add x12, other arithmetic, exit_wave(): real_part * sine_part + imag_part * cosine  13 us
  transfers between devices with their start and end apart: 20, of which 20 were waited for; matrix products, arithmetic and copies ran while one was open for 1% of the time, Pallas kernels for 0%

profile of v1, /device:TPU:0, one launch (start us, length us, event | category | flops | bytes accessed | tf_op | source)
XLA Modules:
  0.0 607.5 jit_solution(5170646944884146478)
XLA Ops:
  7.4 4.9 collective-permute-start
  19.1 9.2 %collective-permute-done.2 = f32[2,32,1280]{2,1,0:T(8,128)S(1)} collective-permute-done((f32[2,32,1280]{2,1,0:T(8,128)S(1)}, f32[2,32,1280]{2,1,0:T(8,128)S(1)}, u32[]{:S(2)}, u32[]{:S(2)}) %collective-permute-start.2) | collective-permute-done | bytes 327712 | tf_op jit(solution)/shard_map/ppermute | solution.py:96
  28.3 9.2 %collective-permute-done.3 = f32[2,32,1280]{2,1,0:T(8,128)S(1)} collective-permute-done((f32[2,32,1280]{2,1,0:T(8,128)S(1)}, f32[2,32,1280]{2,1,0:T(8,128)S(1)}, u32[]{:S(2)}, u32[]{:S(2)}) %collective-permute-start.3) | collective-permute-done | bytes 327712 | tf_op jit(solution)/shard_map/ppermute | solution.py:96
  37.5 9.2 %collective-permute-done.4 = f32[2,32,1280]{2,1,0:T(8,128)S(1)} collective-permute-done((f32[2,32,1280]{2,1,0:T(8,128)S(1)}, f32[2,32,1280]{2,1,0:T(8,128)S(1)}, u32[]{:S(2)}, u32[]{:S(2)}) %collective-permute-start.4) | collective-permute-done | bytes 327712 | tf_op jit(solution)/shard_map/ppermute | solution.py:96
  46.7 9.2 %collective-permute-done.5 = f32[2,32,1280]{2,1,0:T(8,128)S(1)} collective-permute-done((f32[2,32,1280]{2,1,0:T(8,128)S(1)}, f32[2,32,1280]{2,1,0:T(8,128)S(1)}, u32[]{:S(2)}, u32[]{:S(2)}) %collective-permute-start.5) | collective-permute-done | bytes 327712 | tf_op jit(solution)/shard_map/ppermute | solution.py:96
  55.9 9.2 %collective-permute-done.6 = f32[2,32,1280]{2,1,0:T(8,128)S(1)} collective-permute-done((f32[2,32,1280]{2,1,0:T(8,128)S(1)}, f32[2,32,1280]{2,1,0:T(8,128)S(1)}, u32[]{:S(2)}, u32[]{:S(2)}) %collective-permute-start.6) | collective-permute-done | bytes 327712 | tf_op jit(solution)/shard_map/ppermute | solution.py:96
  65.1 9.2 %collective-permute-done.7 = f32[2,32,1280]{2,1,0:T(8,128)S(1)} collective-permute-done((f32[2,32,1280]{2,1,0:T(8,128)S(1)}, f32[2,32,1280]{2,1,0:T(8,128)S(1)}, u32[]{:S(2)}, u32[]{:S(2)}) %collective-permute-start.7) | collective-permute-done | bytes 327712 | tf_op jit(solution)/shard_map/ppermute | solution.py:96
  74.3 9.2 %collective-permute-done.8 = f32[2,32,1280]{2,1,0:T(8,128)S(1)} collective-permute-done((f32[2,32,1280]{2,1,0:T(8,128)S(1)}, f32[2,32,1280]{2,1,0:T(8,128)S(1)}, u32[]{:S(2)}, u32[]{:S(2)}) %collective-permute-start.8) | collective-permute-done | bytes 327712 | tf_op jit(solution)/shard_map/ppermute | solution.py:96
  83.5 9.2 %collective-permute-done.9 = f32[2,32,1280]{2,1,0:T(8,128)S(1)} collective-permute-done((f32[2,32,1280]{2,1,0:T(8,128)S(1)}, f32[2,32,1280]{2,1,0:T(8,128)S(1)}, u32[]{:S(2)}, u32[]{:S(2)}) %collective-permute-start.9) | collective-permute-done | bytes 327712 | tf_op jit(solution)/shard_map/ppermute | solution.py:96
  92.7 9.2 %collective-permute-done.10 = f32[2,32,1280]{2,1,0:T(8,128)S(1)} collective-permute-done((f32[2,32,1280]{2,1,0:T(8,128)S(1)}, f32[2,32,1280]{2,1,0:T(8,128)S(1)}, u32[]{:S(2)}, u32[]{:S(2)}) %collective-permute-start.10) | collective-permute-done | bytes 327712 | tf_op jit(solution)/shard_map/ppermute | solution.py:96
  101.9 9.2 %collective-permute-done.11 = f32[2,32,1280]{2,1,0:T(8,128)S(1)} collective-permute-done((f32[2,32,1280]{2,1,0:T(8,128)S(1)}, f32[2,32,1280]{2,1,0:T(8,128)S(1)}, u32[]{:S(2)}, u32[]{:S(2)}) %collective-permute-start.11) | collective-permute-done | bytes 327712 | tf_op jit(solution)/shard_map/ppermute | solution.py:96
  111.8 9.2 %collective-permute-done.12 = f32[2,32,1280]{2,1,0:T(8,128)S(1)} collective-permute-done((f32[2,32,1280]{2,1,0:T(8,128)S(1)}, f32[2,32,1280]{2,1,0:T(8,128)S(1)}, u32[]{:S(2)}, u32[]{:S(2)}) %collective-permute-start.12) | collective-permute-done | bytes 327712 | tf_op jit(solution)/shard_map/ppermute | solution.py:96
  121.7 9.2 %collective-permute-done.13 = f32[2,32,1280]{2,1,0:T(8,128)S(1)} collective-permute-done((f32[2,32,1280]{2,1,0:T(8,128)S(1)}, f32[2,32,1280]{2,1,0:T(8,128)S(1)}, u32[]{:S(2)}, u32[]{:S(2)}) %collective-permute-start.13) | collective-permute-done | bytes 327712 | tf_op jit(solution)/shard_map/ppermute | solution.py:96
  131.6 9.2 %collective-permute-done.14 = f32[2,32,1280]{2,1,0:T(8,128)S(1)} collective-permute-done((f32[2,32,1280]{2,1,0:T(8,128)S(1)}, f32[2,32,1280]{2,1,0:T(8,128)S(1)}, u32[]{:S(2)}, u32[]{:S(2)}) %collective-permute-start.14) | collective-permute-done | bytes 327712 | tf_op jit(solution)/shard_map/ppermute | solution.py:96
  141.6 9.3 %collective-permute-done.15 = f32[2,32,1280]{2,1,0:T(8,128)} collective-permute-done((f32[2,32,1280]{2,1,0:T(8,128)S(1)}, f32[2,32,1280]{2,1,0:T(8,128)}, u32[]{:S(2)}, u32[]{:S(2)}) %collective-permute-start.15) | collective-permute-done | bytes 327712 | tf_op jit(solution)/shard_map/ppermute | solution.py:96
  152.2 8.2 %collective-permute-done.16 = f32[2,32,1280]{2,1,0:T(8,128)} collective-permute-done((f32[2,32,1280]{2,1,0:T(8,128)}, f32[2,32,1280]{2,1,0:T(8,128)}, u32[]{:S(2)}, u32[]{:S(2)}) %collective-permute-start.16) | collective-permute-done | bytes 327712 | tf_op jit(solution)/shard_map/ppermute | solution.py:96
  175.7 340.2 %while.17 = (s32[]{:T(128)}, f32[2,512,1280]{2,1,0:T(8,128)}, s32[]{:T(128)}, s32[1,1,6]{2,1,0:T(1,128)S(1)}, s32[1,2,96]{2,1,0:T(2,128)S(1)}, /*index=5*/f32[2,...) while((s32[]{:T(128)}, f32[2,512,1280]{2,1,0:T(8,128)}, ...), condition=%wide.region_1.2_spmd.clone.clone, body=%wide.region_0.1_spmd.clone.clone.sunk | while | flops 3259498496 | bytes 60293488 | solution.py:122
  243.7 6.6 %dynamic_update_slice.10 = f32[2,512,1280]{2,1,0:T(8,128)} dynamic-update-slice(f32[2,512,1280]{2,1,0:T(8,128)} %get-tuple-element.599, f32[2,256,256]{2,1,0:T(8,128)S(1)} %copy.34, s32[]{:T(128)} %constant.267.clone.1..sunk, s32[]{:T(128)S(6)} %select_n.171, s32[]{:T(128)S(6)} %select_n.172) | dynamic-update-slice | bytes 1048580 | tf_op jit(solution)/shard_map/while/body/dynamic_update_slice | solution.py:118
  296.7 6.4 %dynamic_update_slice.10 = f32[2,512,1280]{2,1,0:T(8,128)} dynamic-update-slice(f32[2,512,1280]{2,1,0:T(8,128)} %get-tuple-element.599, f32[2,256,256]{2,1,0:T(8,128)S(1)} %copy.34, s32[]{:T(128)} %constant.267.clone.1..sunk, s32[]{:T(128)S(6)} %select_n.171, s32[]{:T(128)S(6)} %select_n.172) | dynamic-update-slice | bytes 1048580 | tf_op jit(solution)/shard_map/while/body/dynamic_update_slice | solution.py:118
  349.6 6.1 %dynamic_update_slice.10 = f32[2,512,1280]{2,1,0:T(8,128)} dynamic-update-slice(f32[2,512,1280]{2,1,0:T(8,128)} %get-tuple-element.599, f32[2,256,256]{2,1,0:T(8,128)S(1)} %copy.34, s32[]{:T(128)} %constant.267.clone.1..sunk, s32[]{:T(128)S(6)} %select_n.171, s32[]{:T(128)S(6)} %select_n.172) | dynamic-update-slice | bytes 1048580 | tf_op jit(solution)/shard_map/while/body/dynamic_update_slice | solution.py:118
  402.2 6.7 %dynamic_update_slice.10 = f32[2,512,1280]{2,1,0:T(8,128)} dynamic-update-slice(f32[2,512,1280]{2,1,0:T(8,128)} %get-tuple-element.599, f32[2,256,256]{2,1,0:T(8,128)S(1)} %copy.34, s32[]{:T(128)} %constant.267.clone.1..sunk, s32[]{:T(128)S(6)} %select_n.171, s32[]{:T(128)S(6)} %select_n.172) | dynamic-update-slice | bytes 1048580 | tf_op jit(solution)/shard_map/while/body/dynamic_update_slice | solution.py:118
  455.4 6.5 %dynamic_update_slice.10 = f32[2,512,1280]{2,1,0:T(8,128)} dynamic-update-slice(f32[2,512,1280]{2,1,0:T(8,128)} %get-tuple-element.599, f32[2,256,256]{2,1,0:T(8,128)S(1)} %copy.34, s32[]{:T(128)} %constant.267.clone.1..sunk, s32[]{:T(128)S(6)} %select_n.171, s32[]{:T(128)S(6)} %select_n.172) | dynamic-update-slice | bytes 1048580 | tf_op jit(solution)/shard_map/while/body/dynamic_update_slice | solution.py:118
  508.3 6.7 %dynamic_update_slice.10 = f32[2,512,1280]{2,1,0:T(8,128)} dynamic-update-slice(f32[2,512,1280]{2,1,0:T(8,128)} %get-tuple-element.599, f32[2,256,256]{2,1,0:T(8,128)S(1)} %copy.34, s32[]{:T(128)} %constant.267.clone.1..sunk, s32[]{:T(128)S(6)} %select_n.171, s32[]{:T(128)S(6)} %select_n.172) | dynamic-update-slice | bytes 1048580 | tf_op jit(solution)/shard_map/while/body/dynamic_update_slice | solution.py:118
  531.5 68.8 %reduce-scatter.2.cloned.1.call-done = f32[2,32,1024]{2,1,0:T(8,128)} async-done(((f32[2,512,1024]{2,1,0:T(8,128)}), f32[2,32,1024]{2,1,0:T(8,128)}) %reduce-scatter.2.cloned.1.call-update) | async-done | bytes 262160 | tf_op jit(solution)/shard_map/reduce_scatter | solution.py:126
  (419 shorter events, 284.7 us)
Async XLA Ops:
  6.5 161.1 %copy-start = (f32[2,32,1024]{2,1,0:T(8,128)S(1)}, f32[2,32,1024]{2,1,0:T(8,128)}, u32[]{:S(2)}) copy-start(f32[2,32,1024]{2,1,0:T(8,128)} %param.12) | copy-start | bytes 786436
  6.5 593.8 %reduce-scatter.2.cloned.1.call-start = ((), (), s32[]{:S(2)}) async-start(), calls=%async_computation.1 | async-start | bytes 4456448 | tf_op jit(solution)/shard_map/reduce_scatter | solution.py:126
  7.4 6.4 %collective-permute-start = (f32[2,32,128]{2,1,0:T(8,128)S(1)}, f32[2,32,128]{2,1,0:T(8,128)S(1)}, u32[]{:S(2)}, u32[]{:S(2)}) collective-permute-start(f32[2,32,128]{2,1,0:T(8,128)S(1)} %get-tuple-element.418), channel_id=1, source_target_pairs={{0,1},{2,3},{4,5},{6,7},{8,9},{10,11},{12,13},{14,15},{16,17},{18,... | collective-permute-start | bytes 98312 | tf_op jit(solution)/shard_map/ppermute | solution.py:19
  12.2 5.8 collective-permute-start.1
  19.0 9.2 %collective-permute-start.2 = (f32[2,32,1280]{2,1,0:T(8,128)S(1)}, f32[2,32,1280]{2,1,0:T(8,128)S(1)}, u32[]{:S(2)}, u32[]{:S(2)}) collective-permute-start(f32[2,32,1280]{2,1,0:T(8,128)S(1)} %pad_maximum_fusion), channel_id=1, source_target_pairs={{0,2},{2,4},{4,6},{6,8},{8,10},{10,12},{12,14},{14,16},{16,18},{18... | collective-permute-start | bytes 983048 | tf_op jit(solution)/shard_map/ppermute | solution.py:96
  28.3 9.2 %collective-permute-start.3 = (f32[2,32,1280]{2,1,0:T(8,128)S(1)}, f32[2,32,1280]{2,1,0:T(8,128)S(1)}, u32[]{:S(2)}, u32[]{:S(2)}) collective-permute-start(f32[2,32,1280]{2,1,0:T(8,128)S(1)} %collective-permute-done.2), channel_id=1, source_target_pairs={{0,2},{2,4},{4,6},{6,8},{8,10},{10,12},{12,14},{14,16},{16,18},{18... | collective-permute-start | bytes 983048 | tf_op jit(solution)/shard_map/ppermute | solution.py:96
  37.5 9.2 %collective-permute-start.4 = (f32[2,32,1280]{2,1,0:T(8,128)S(1)}, f32[2,32,1280]{2,1,0:T(8,128)S(1)}, u32[]{:S(2)}, u32[]{:S(2)}) collective-permute-start(f32[2,32,1280]{2,1,0:T(8,128)S(1)} %collective-permute-done.3), channel_id=1, source_target_pairs={{0,2},{2,4},{4,6},{6,8},{8,10},{10,12},{12,14},{14,16},{16,18},{18... | collective-permute-start | bytes 983048 | tf_op jit(solution)/shard_map/ppermute | solution.py:96
  46.7 9.2 %collective-permute-start.5 = (f32[2,32,1280]{2,1,0:T(8,128)S(1)}, f32[2,32,1280]{2,1,0:T(8,128)S(1)}, u32[]{:S(2)}, u32[]{:S(2)}) collective-permute-start(f32[2,32,1280]{2,1,0:T(8,128)S(1)} %collective-permute-done.4), channel_id=1, source_target_pairs={{0,2},{2,4},{4,6},{6,8},{8,10},{10,12},{12,14},{14,16},{16,18},{18... | collective-permute-start | bytes 983048 | tf_op jit(solution)/shard_map/ppermute | solution.py:96
  55.9 9.2 %collective-permute-start.6 = (f32[2,32,1280]{2,1,0:T(8,128)S(1)}, f32[2,32,1280]{2,1,0:T(8,128)S(1)}, u32[]{:S(2)}, u32[]{:S(2)}) collective-permute-start(f32[2,32,1280]{2,1,0:T(8,128)S(1)} %collective-permute-done.5), channel_id=1, source_target_pairs={{0,2},{2,4},{4,6},{6,8},{8,10},{10,12},{12,14},{14,16},{16,18},{18... | collective-permute-start | bytes 983048 | tf_op jit(solution)/shard_map/ppermute | solution.py:96
  65.1 9.2 %collective-permute-start.7 = (f32[2,32,1280]{2,1,0:T(8,128)S(1)}, f32[2,32,1280]{2,1,0:T(8,128)S(1)}, u32[]{:S(2)}, u32[]{:S(2)}) collective-permute-start(f32[2,32,1280]{2,1,0:T(8,128)S(1)} %collective-permute-done.6), channel_id=1, source_target_pairs={{0,2},{2,4},{4,6},{6,8},{8,10},{10,12},{12,14},{14,16},{16,18},{18... | collective-permute-start | bytes 983048 | tf_op jit(solution)/shard_map/ppermute | solution.py:96
  74.3 9.2 %collective-permute-start.8 = (f32[2,32,1280]{2,1,0:T(8,128)S(1)}, f32[2,32,1280]{2,1,0:T(8,128)S(1)}, u32[]{:S(2)}, u32[]{:S(2)}) collective-permute-start(f32[2,32,1280]{2,1,0:T(8,128)S(1)} %collective-permute-done.7), channel_id=1, source_target_pairs={{0,2},{2,4},{4,6},{6,8},{8,10},{10,12},{12,14},{14,16},{16,18},{18... | collective-permute-start | bytes 983048 | tf_op jit(solution)/shard_map/ppermute | solution.py:96
  83.5 9.2 %collective-permute-start.9 = (f32[2,32,1280]{2,1,0:T(8,128)S(1)}, f32[2,32,1280]{2,1,0:T(8,128)S(1)}, u32[]{:S(2)}, u32[]{:S(2)}) collective-permute-start(f32[2,32,1280]{2,1,0:T(8,128)S(1)} %collective-permute-done.8), channel_id=1, source_target_pairs={{0,2},{2,4},{4,6},{6,8},{8,10},{10,12},{12,14},{14,16},{16,18},{18... | collective-permute-start | bytes 983048 | tf_op jit(solution)/shard_map/ppermute | solution.py:96
  92.7 9.2 %collective-permute-start.10 = (f32[2,32,1280]{2,1,0:T(8,128)S(1)}, f32[2,32,1280]{2,1,0:T(8,128)S(1)}, u32[]{:S(2)}, u32[]{:S(2)}) collective-permute-start(f32[2,32,1280]{2,1,0:T(8,128)S(1)} %collective-permute-done.9), channel_id=1, source_target_pairs={{0,2},{2,4},{4,6},{6,8},{8,10},{10,12},{12,14},{14,16},{16,18},{18... | collective-permute-start | bytes 983048 | tf_op jit(solution)/shard_map/ppermute | solution.py:96
  101.9 49.0 %copy-start.1 = (f32[2,32,1280]{2,1,0:T(8,128)}, f32[2,32,1280]{2,1,0:T(8,128)S(1)}, u32[]{:S(2)}) copy-start(f32[2,32,1280]{2,1,0:T(8,128)S(1)} %collective-permute-done.10) | copy-start | bytes 983044
  101.9 9.2 %collective-permute-start.11 = (f32[2,32,1280]{2,1,0:T(8,128)S(1)}, f32[2,32,1280]{2,1,0:T(8,128)S(1)}, u32[]{:S(2)}, u32[]{:S(2)}) collective-permute-start(f32[2,32,1280]{2,1,0:T(8,128)S(1)} %collective-permute-done.10), channel_id=1, source_target_pairs={{0,2},{2,4},{4,6},{6,8},{8,10},{10,12},{12,14},{14,16},{16,18},{18... | collective-permute-start | bytes 983048 | tf_op jit(solution)/shard_map/ppermute | solution.py:96
  111.8 9.2 %collective-permute-start.12 = (f32[2,32,1280]{2,1,0:T(8,128)S(1)}, f32[2,32,1280]{2,1,0:T(8,128)S(1)}, u32[]{:S(2)}, u32[]{:S(2)}) collective-permute-start(f32[2,32,1280]{2,1,0:T(8,128)S(1)} %collective-permute-done.11), channel_id=1, source_target_pairs={{0,2},{2,4},{4,6},{6,8},{8,10},{10,12},{12,14},{14,16},{16,18},{18... | collective-permute-start | bytes 983048 | tf_op jit(solution)/shard_map/ppermute | solution.py:96
  121.7 9.2 %collective-permute-start.13 = (f32[2,32,1280]{2,1,0:T(8,128)S(1)}, f32[2,32,1280]{2,1,0:T(8,128)S(1)}, u32[]{:S(2)}, u32[]{:S(2)}) collective-permute-start(f32[2,32,1280]{2,1,0:T(8,128)S(1)} %collective-permute-done.12), channel_id=1, source_target_pairs={{0,2},{2,4},{4,6},{6,8},{8,10},{10,12},{12,14},{14,16},{16,18},{18... | collective-permute-start | bytes 983048 | tf_op jit(solution)/shard_map/ppermute | solution.py:96
  131.6 9.2 %collective-permute-start.14 = (f32[2,32,1280]{2,1,0:T(8,128)S(1)}, f32[2,32,1280]{2,1,0:T(8,128)S(1)}, u32[]{:S(2)}, u32[]{:S(2)}) collective-permute-start(f32[2,32,1280]{2,1,0:T(8,128)S(1)} %collective-permute-done.13), channel_id=1, source_target_pairs={{0,2},{2,4},{4,6},{6,8},{8,10},{10,12},{12,14},{14,16},{16,18},{18... | collective-permute-start | bytes 983048 | tf_op jit(solution)/shard_map/ppermute | solution.py:96
  141.6 9.3 %collective-permute-start.15 = (f32[2,32,1280]{2,1,0:T(8,128)S(1)}, f32[2,32,1280]{2,1,0:T(8,128)}, u32[]{:S(2)}, u32[]{:S(2)}) collective-permute-start(f32[2,32,1280]{2,1,0:T(8,128)S(1)} %collective-permute-done.14), channel_id=1, source_target_pairs={{0,2},{2,4},{4,6},{6,8},{8,10},{10,12},{12,14},{14,16},{16,18},{18... | collective-permute-start | bytes 983048 | tf_op jit(solution)/shard_map/ppermute | solution.py:96
  150.9 9.5 %collective-permute-start.16 = (f32[2,32,1280]{2,1,0:T(8,128)}, f32[2,32,1280]{2,1,0:T(8,128)}, u32[]{:S(2)}, u32[]{:S(2)}) collective-permute-start(f32[2,32,1280]{2,1,0:T(8,128)} %collective-permute-done.15), channel_id=1, source_target_pairs={{0,2},{2,4},{4,6},{6,8},{8,10},{10,12},{12,14},{14,16},{16,18},{18... | collective-permute-start | bytes 983048 | tf_op jit(solution)/shard_map/ppermute | solution.py:96
  152.2 17.7 %copy-start.4 = (f32[2,32,1280]{2,1,0:T(8,128)S(1)}, f32[2,32,1280]{2,1,0:T(8,128)}, u32[]{:S(2)}) copy-start(f32[2,32,1280]{2,1,0:T(8,128)} %copy-done.3) | copy-start | bytes 983044
  152.2 17.7 %copy-start.2 = (f32[2,32,1280]{2,1,0:T(8,128)S(1)}, f32[2,32,1280]{2,1,0:T(8,128)}, u32[]{:S(2)}) copy-start(f32[2,32,1280]{2,1,0:T(8,128)} %copy-done.1) | copy-start | bytes 983044
  517.2 8.0 %collective-permute-start.17 = (f32[2,512,128]{2,1,0:T(8,128)S(1)}, f32[2,512,128]{2,1,0:T(8,128)S(1)}, u32[]{:S(2)}, u32[]{:S(2)}) collective-permute-start(f32[2,512,128]{2,1,0:T(8,128)S(1)} %get-tuple-element.417), channel_id=1, source_target_pairs={{0,1},{2,3},{4,5},{6,7},{8,9},{10,11},{12,13},{14,15},{16,17},{18,... | collective-permute-start | bytes 1572872 | tf_op jit(solution)/shard_map/ppermute | solution.py:19
  518.5 11.1 %collective-permute-start.18 = (f32[2,512,128]{2,1,0:T(8,128)S(1)}, f32[2,512,128]{2,1,0:T(8,128)S(1)}, u32[]{:S(2)}, u32[]{:S(2)}) collective-permute-start(f32[2,512,128]{2,1,0:T(8,128)S(1)} %get-tuple-element.416), channel_id=1, source_target_pairs={{1,0},{3,2},{5,4},{7,6},{9,8},{11,10},{13,12},{15,14},{17,16},{19,... | collective-permute-start | bytes 1572872 | tf_op jit(solution)/shard_map/ppermute | solution.py:20
  (9 other events, 67.2 us)
Sparse Core Ops, SparseCore 0:
  531.6 68.6 reduce-scatter.1
